TPU v7x, 512 devices: a whole 4x8x8 slice. The times are simulated.
512 devices in a mesh: seq: 64 (over y_lo, x, z), head: 8 (over y_hi, core).
Axes of the slice: x: 4, y: 8 (y_hi: 4, y_lo: 2; y = y_hi * 2 + y_lo), z: 8, core: 2. Of those that a mesh axis runs over, the one named last changes fastest.
Arguments:
- queries: bfloat16 [16384, 3072], P(('seq', 'head')), may hold values from -6 to 6
- keys: bfloat16 [16384, 3072], P('seq', 'head'), may hold values from -6 to 6
- values: bfloat16 [16384, 3072], P('seq', 'head'), may hold values from -6 to 6
- window: int32 [64, 27], P('seq'), may hold values from -1 to 63, as said below
- out_weight: bfloat16 [3072, 6144], P('seq', 'head'), may hold values from -0.109375 to 0.109375
Outputs:
- projected: bfloat16 [16384, 6144], P('seq', 'head')
Inputs may be any that keep to these rules, and one draw needn't show every extreme that they name: Tile g lies at (g // 16, g // 4 % 4, g % 4) in a grid of 4 x 4 x 4 tiles. Entry k of window[g] is either -1 or the tile that lies (k // 9 - 1, k // 3 % 3 - 1, k % 3 - 1) steps away from g along time, height and width; it is -1 where that tile is outside the grid. Entry 13 is g itself.
All inputs are finite; a program needn't handle non-finite values.
Results may differ from a plain program's by a relative error of at most 0.0075.
Values may be sent and summed in bfloat16 or wider, within the bound.
A program may use at most 64 MiB of HBM per device.

v0:
```python
import jax
import jax.numpy as jnp
from jax import lax
from jax.sharding import PartitionSpec as P

HEAD_DIM = 128
GH = 4
GW = 4


def passed_along(array, axis, by):
    count = lax.axis_size(axis)
    pairs = [(i, i + by) for i in range(count) if 0 <= i + by < count]
    return lax.ppermute(array, axis, pairs)


def attend_block(softmax_state, queries, kv_block, live_keys):
    run_max, run_sum, run_acc = softmax_state
    factor = queries.shape[-1] ** (-0.5)
    scores = (
        jnp.einsum("qhd,khd->qhk", queries, kv_block[0], preferred_element_type=jnp.float32)
        * factor
    )
    scores = jnp.where(live_keys[None, None, :], scores, -1e30)
    new_max = jnp.maximum(run_max, jnp.max(scores, axis=-1))
    rescale = jnp.exp(run_max - new_max)
    weights = jnp.where(live_keys[None, None, :], jnp.exp(scores - new_max[:, :, None]), 0.0)
    run_sum = run_sum * rescale + jnp.sum(weights, axis=-1)
    run_acc = run_acc * rescale[:, :, None] + jnp.einsum(
        "qhk,khd->qhd",
        weights.astype(jnp.bfloat16),
        kv_block[1],
        preferred_element_type=jnp.float32,
    )
    return (new_max, run_sum, run_acc)


def local(queries, keys, values, window, out_weight):
    tok_rows = queries.shape[0]
    head_width = HEAD_DIM
    heads_all = queries.shape[1] // head_width
    local_q = lax.all_to_all(
        queries.reshape(tok_rows, heads_all, head_width),
        "head",
        split_axis=1,
        concat_axis=0,
        tiled=True,
    )
    tile_rows = local_q.shape[0]
    heads_dev = local_q.shape[1]
    live_tiles = window[0] >= 0
    kv_pair = jnp.stack(
        [
            keys.reshape(tile_rows, heads_dev, head_width),
            values.reshape(tile_rows, heads_dev, head_width),
        ]
    )
    softmax_state = (
        jnp.full((tile_rows, heads_dev), -1e30, jnp.float32),
        jnp.zeros((tile_rows, heads_dev), jnp.float32),
        jnp.zeros((tile_rows, heads_dev, head_width), jnp.float32),
    )
    seq_span = lax.axis_size("seq")
    plane_size = GH * GW

    def tile_mask(first_slot, tile_count):
        return jnp.repeat(live_tiles[first_slot : first_slot + tile_count], tile_rows)

    softmax_state = attend_block(softmax_state, local_q, kv_pair, tile_mask(13, 1))
    for slot_index in range(27):
        offset = (
            (slot_index // 9 - 1) * plane_size
            + (slot_index // 3 % 3 - 1) * GW
            + (slot_index % 3 - 1)
        )
        if slot_index != 13 and abs(offset) < seq_span:
            remote = passed_along(kv_pair, "seq", -offset)
            softmax_state = attend_block(softmax_state, local_q, remote, tile_mask(slot_index, 1))
    run_max, run_sum, run_acc = softmax_state
    finished = (run_acc / run_sum[:, :, None]).astype(jnp.bfloat16)
    finished = finished.reshape(tile_rows, heads_dev * head_width)
    all_heads = lax.all_gather(finished, "head", axis=1, tiled=True)
    projected = jnp.dot(
        all_heads,
        lax.all_gather(out_weight, "seq", axis=0, tiled=True),
        preferred_element_type=jnp.float32,
    )
    return projected.astype(jnp.bfloat16)


def solution(mesh):
    in_specs = (
        P(("seq", "head"), None),
        P("seq", "head"),
        P("seq", "head"),
        P("seq", None),
        P("seq", "head"),
    )
    out_specs = P("seq", "head")
    return jax.shard_map(local, mesh=mesh, in_specs=in_specs, out_specs=out_specs, check_vma=False)
```

profile of v0, /device:TPU:16, one launch (start us, length us, event | category | flops | bytes accessed | tf_op | source)
XLA Modules:
  0.0 854.9 jit_solution(16147548756407061988)
XLA Ops:
  6.5 1.1 copy.188
  7.8 1.1 copy.184
  9.1 1.3 collective-permute-start.25
  10.4 1.3 collective-permute-start.24
  11.7 1.3 collective-permute-start.23
  13.0 1.3 collective-permute-start.22
  14.3 1.3 collective-permute-start.21
  16.3 9.0 %all-to-all-start = ((bf16[32,24,128]{2,0,1:T(8,128)(2,1)}), bf16[32,24,128]{2,0,1:T(8,128)(2,1)S(1)}, u32[]{:S(2)}, u32[]{:S(2)}) async-start(bf16[32,24,128]{2,0,1:T(8,128)(2,1)} %copy_bitcast_fusion), calls=%async_computation | async-start | bytes 393216 | tf_op jit(solution)/shard_map/all_to_all | solution.py:42
  27.4 5.1 all-to-all-done
  34.1 18.8 %collective-permute-done.25 = bf16[2,256,3,128]{3,1,2,0:T(8,128)(2,1)S(1)} collective-permute-done((bf16[2,256,3,128]{3,1,2,0:T(8,128)(2,1)S(1)}, bf16[2,256,3,128]{3,1,2,0:T(8,128)(2,1)S(1)}, u32[]{:S(2)}, u32[]{:S(2)}) %collective-permute-start.25) | collective-permute-done | bytes 393248 | tf_op jit(solution)/shard_map/ppermute | solution.py:14
  52.9 1.3 collective-permute-start.20
  54.2 1.0 fusion.303
  55.1 6.6 collective-permute-done.24
  61.7 1.3 collective-permute-start.19
  63.9 1.3 collective-permute-start.18
  66.1 1.3 collective-permute-start.17
  68.4 1.3 collective-permute-start.16
  70.6 50.1 %collective-permute-done.20 = bf16[2,256,3,128]{3,1,2,0:T(8,128)(2,1)S(1)} collective-permute-done((bf16[2,256,3,128]{3,1,2,0:T(8,128)(2,1)S(1)}, bf16[2,256,3,128]{3,1,2,0:T(8,128)(2,1)S(1)}, u32[]{:S(2)}, u32[]{:S(2)}) %collective-permute-start.20) | collective-permute-done | bytes 393248 | tf_op jit(solution)/shard_map/ppermute | solution.py:14
  120.7 1.3 collective-permute-start.15
  122.8 1.3 collective-permute-start.14
  125.0 1.3 collective-permute-start.13
  127.2 44.3 %collective-permute-start.12 = (bf16[2,256,3,128]{3,1,2,0:T(8,128)(2,1)S(1)}, bf16[2,256,3,128]{3,1,2,0:T(8,128)(2,1)S(1)}, u32[]{:S(2)}, u32[]{:S(2)}) collective-permute-start(bf16[2,256,3,128]{3,1,2,0:T(8,128)(2,1)S(1)} %pad_maximum_fusion), channel_id=1, source_target_pairs={{0,8},{8,16},{16,24},{24,32},{32,40},{40,48},{48,56},{56,64},{64,7... | collective-permute-start | bytes 1179656 | tf_op jit(solution)/shard_map/ppermute | solution.py:14
  172.5 36.7 %collective-permute-start.11 = (bf16[2,256,3,128]{3,1,2,0:T(8,128)(2,1)S(1)}, bf16[2,256,3,128]{3,1,2,0:T(8,128)(2,1)S(1)}, u32[]{:S(2)}, u32[]{:S(2)}) collective-permute-start(bf16[2,256,3,128]{3,1,2,0:T(8,128)(2,1)S(1)} %pad_maximum_fusion), channel_id=1, source_target_pairs={{0,24},{8,32},{16,40},{24,48},{32,56},{40,64},{48,72},{56,80},{64,... | collective-permute-start | bytes 1179656 | tf_op jit(solution)/shard_map/ppermute | solution.py:14
  210.1 13.1 %collective-permute-done.15 = bf16[2,256,3,128]{3,1,2,0:T(8,128)(2,1)S(1)} collective-permute-done((bf16[2,256,3,128]{3,1,2,0:T(8,128)(2,1)S(1)}, bf16[2,256,3,128]{3,1,2,0:T(8,128)(2,1)S(1)}, u32[]{:S(2)}, u32[]{:S(2)}) %collective-permute-start.15) | collective-permute-done | bytes 393248 | tf_op jit(solution)/shard_map/ppermute | solution.py:14
  223.2 15.7 %collective-permute-start.10 = (bf16[2,256,3,128]{3,1,2,0:T(8,128)(2,1)S(1)}, bf16[2,256,3,128]{3,1,2,0:T(8,128)(2,1)S(1)}, u32[]{:S(2)}, u32[]{:S(2)}) collective-permute-start(bf16[2,256,3,128]{3,1,2,0:T(8,128)(2,1)S(1)} %pad_maximum_fusion), channel_id=1, source_target_pairs={{0,32},{8,40},{16,48},{24,56},{32,64},{40,72},{48,80},{56,88},{64,... | collective-permute-start | bytes 1179656 | tf_op jit(solution)/shard_map/ppermute | solution.py:14
  238.9 1.0 fusion.313
  239.8 1.3 collective-permute-start.9
  241.2 1.0 fusion.314
  242.2 1.3 collective-permute-start.8
  244.3 14.4 %collective-permute-start.7 = (bf16[2,256,3,128]{3,1,2,0:T(8,128)(2,1)S(1)}, bf16[2,256,3,128]{3,1,2,0:T(8,128)(2,1)S(1)}, u32[]{:S(2)}, u32[]{:S(2)}) collective-permute-start(bf16[2,256,3,128]{3,1,2,0:T(8,128)(2,1)S(1)} %pad_maximum_fusion), channel_id=1, source_target_pairs={{0,96},{8,104},{16,112},{24,120},{32,128},{40,136},{48,144},{56,15... | collective-permute-start | bytes 1179656 | tf_op jit(solution)/shard_map/ppermute | solution.py:14
  259.6 19.4 %collective-permute-start.6 = (bf16[2,256,3,128]{3,1,2,0:T(8,128)(2,1)S(1)}, bf16[2,256,3,128]{3,1,2,0:T(8,128)(2,1)S(1)}, u32[]{:S(2)}, u32[]{:S(2)}) collective-permute-start(bf16[2,256,3,128]{3,1,2,0:T(8,128)(2,1)S(1)} %pad_maximum_fusion), channel_id=1, source_target_pairs={{0,104},{8,112},{16,120},{24,128},{32,136},{40,144},{48,152},{56,1... | collective-permute-start | bytes 1179656 | tf_op jit(solution)/shard_map/ppermute | solution.py:14
  279.9 1.3 collective-permute-start.5
  282.2 16.3 %collective-permute-done.9 = bf16[2,256,3,128]{3,1,2,0:T(8,128)(2,1)S(1)} collective-permute-done((bf16[2,256,3,128]{3,1,2,0:T(8,128)(2,1)S(1)}, bf16[2,256,3,128]{3,1,2,0:T(8,128)(2,1)S(1)}, u32[]{:S(2)}, u32[]{:S(2)}) %collective-permute-start.9) | collective-permute-done | bytes 393248 | tf_op jit(solution)/shard_map/ppermute | solution.py:14
  298.4 29.9 %collective-permute-start.4 = (bf16[2,256,3,128]{3,1,2,0:T(8,128)(2,1)S(1)}, bf16[2,256,3,128]{3,1,2,0:T(8,128)(2,1)S(1)}, u32[]{:S(2)}, u32[]{:S(2)}) collective-permute-start(bf16[2,256,3,128]{3,1,2,0:T(8,128)(2,1)S(1)} %pad_maximum_fusion), channel_id=1, source_target_pairs={{0,128},{8,136},{16,144},{24,152},{32,160},{40,168},{48,176},{56,1... | collective-permute-start | bytes 1179656 | tf_op jit(solution)/shard_map/ppermute | solution.py:14
  329.3 18.6 %collective-permute-start.3 = (bf16[2,256,3,128]{3,1,2,0:T(8,128)(2,1)S(1)}, bf16[2,256,3,128]{3,1,2,0:T(8,128)(2,1)S(1)}, u32[]{:S(2)}, u32[]{:S(2)}) collective-permute-start(bf16[2,256,3,128]{3,1,2,0:T(8,128)(2,1)S(1)} %pad_maximum_fusion), channel_id=1, source_target_pairs={{0,136},{8,144},{16,152},{24,160},{32,168},{40,176},{48,184},{56,1... | collective-permute-start | bytes 1179656 | tf_op jit(solution)/shard_map/ppermute | solution.py:14
  347.9 1.0 fusion.320
  348.9 4.2 collective-permute-start.2
  354.0 10.9 %collective-permute-start.1 = (bf16[2,256,3,128]{3,1,2,0:T(8,128)(2,1)S(1)}, bf16[2,256,3,128]{3,1,2,0:T(8,128)(2,1)S(1)}, u32[]{:S(2)}, u32[]{:S(2)}) collective-permute-start(bf16[2,256,3,128]{3,1,2,0:T(8,128)(2,1)S(1)} %pad_maximum_fusion), channel_id=1, source_target_pairs={{0,160},{8,168},{16,176},{24,184},{32,192},{40,200},{48,208},{56,2... | collective-permute-start | bytes 1179656 | tf_op jit(solution)/shard_map/ppermute | solution.py:14
  365.8 9.8 %collective-permute-start = (bf16[2,256,3,128]{3,1,2,0:T(8,128)(2,1)S(1)}, bf16[2,256,3,128]{3,1,2,0:T(8,128)(2,1)S(1)}, u32[]{:S(2)}, u32[]{:S(2)}) collective-permute-start(bf16[2,256,3,128]{3,1,2,0:T(8,128)(2,1)S(1)} %pad_maximum_fusion), channel_id=1, source_target_pairs={{0,168},{8,176},{16,184},{24,192},{32,200},{40,208},{48,216},{56,2... | collective-permute-start | bytes 1179656 | tf_op jit(solution)/shard_map/ppermute | solution.py:14
  380.0 1.0 fusion.327
  381.0 21.5 %collective-permute-done = bf16[2,256,3,128]{3,1,2,0:T(8,128)(2,1)S(1)} collective-permute-done((bf16[2,256,3,128]{3,1,2,0:T(8,128)(2,1)S(1)}, bf16[2,256,3,128]{3,1,2,0:T(8,128)(2,1)S(1)}, u32[]{:S(2)}, u32[]{:S(2)}) %collective-permute-start) | collective-permute-done | bytes 393248 | tf_op jit(solution)/shard_map/ppermute | solution.py:14
  402.4 1.0 fusion.328
  403.5 1.6 fusion.159
  405.0 1.5 fusion.155
  406.6 1.5 fusion.151
  408.0 1.5 fusion.147
  409.6 1.5 fusion.143
  411.0 1.7 fusion.139
  412.7 1.5 fusion.135
  414.1 1.5 fusion.131
  415.7 1.6 fusion.127
  417.3 1.5 fusion.123
  418.7 1.5 fusion.119
  420.2 1.5 fusion.115
  421.7 1.7 fusion.111
  424.3 1.0 convolution_bitcast_fusion.1
  433.3 1.0 convolution_bitcast_fusion.11
  434.3 1.0 convolution_bitcast_fusion.12
  439.7 1.0 convolution_bitcast_fusion.18
  445.9 1.0 convolution_bitcast_fusion.25
  446.9 2.5 fusion.108
  450.1 83.4 %all-gather.3.cloned.1.call-done = bf16[256,3072]{0,1:T(8,128)(2,1)} async-done(((bf16[256,384]{0,1:T(8,128)(2,1)}), bf16[256,3072]{0,1:T(8,128)(2,1)}) %all-gather.3.cloned.1.call-update) | async-done | bytes 1572880 | tf_op jit(solution)/shard_map/all_gather | solution.py:82
  533.6 309.5 %all-gather.5.cloned.1.call-done = bf16[3072,768]{1,0:T(8,128)(2,1)} async-done(((bf16[48,768]{1,0:T(8,128)(2,1)}), bf16[3072,768]{1,0:T(8,128)(2,1)}) %all-gather.5.cloned.1.call-update) | async-done | bytes 4718608 | tf_op jit(solution)/shard_map/all_gather | solution.py:85
  843.1 5.0 convolution_convert_fusion
  (80 shorter events, 42.8 us)
Async XLA Ops:
  6.5 9.1 %copy-start = (bf16[32,3072]{1,0:T(8,128)(2,1)S(1)}, bf16[32,3072]{1,0:T(8,128)(2,1)}, u32[]{:S(2)}) copy-start(bf16[32,3072]{1,0:T(8,128)(2,1)} %param.5) | copy-start | bytes 589828
  9.1 43.8 %collective-permute-start.25 = (bf16[2,256,3,128]{3,1,2,0:T(8,128)(2,1)S(1)}, bf16[2,256,3,128]{3,1,2,0:T(8,128)(2,1)S(1)}, u32[]{:S(2)}, u32[]{:S(2)}) collective-permute-start(bf16[2,256,3,128]{3,1,2,0:T(8,128)(2,1)S(1)} %pad_maximum_fusion), channel_id=1, source_target_pairs={{168,0},{176,8},{184,16},{192,24},{200,32},{208,40},{216,48},{224,... | collective-permute-start | bytes 1179656 | tf_op jit(solution)/shard_map/ppermute | solution.py:14
  10.4 51.3 %collective-permute-start.24 = (bf16[2,256,3,128]{3,1,2,0:T(8,128)(2,1)S(1)}, bf16[2,256,3,128]{3,1,2,0:T(8,128)(2,1)S(1)}, u32[]{:S(2)}, u32[]{:S(2)}) collective-permute-start(bf16[2,256,3,128]{3,1,2,0:T(8,128)(2,1)S(1)} %pad_maximum_fusion), channel_id=1, source_target_pairs={{160,0},{168,8},{176,16},{184,24},{192,32},{200,40},{208,48},{216,... | collective-permute-start | bytes 1179656 | tf_op jit(solution)/shard_map/ppermute | solution.py:14
  11.7 52.2 %collective-permute-start.23 = (bf16[2,256,3,128]{3,1,2,0:T(8,128)(2,1)S(1)}, bf16[2,256,3,128]{3,1,2,0:T(8,128)(2,1)S(1)}, u32[]{:S(2)}, u32[]{:S(2)}) collective-permute-start(bf16[2,256,3,128]{3,1,2,0:T(8,128)(2,1)S(1)} %pad_maximum_fusion), channel_id=1, source_target_pairs={{152,0},{160,8},{168,16},{176,24},{184,32},{192,40},{200,48},{208,... | collective-permute-start | bytes 1179656 | tf_op jit(solution)/shard_map/ppermute | solution.py:14
  13.0 53.2 %collective-permute-start.22 = (bf16[2,256,3,128]{3,1,2,0:T(8,128)(2,1)S(1)}, bf16[2,256,3,128]{3,1,2,0:T(8,128)(2,1)S(1)}, u32[]{:S(2)}, u32[]{:S(2)}) collective-permute-start(bf16[2,256,3,128]{3,1,2,0:T(8,128)(2,1)S(1)} %pad_maximum_fusion), channel_id=1, source_target_pairs={{136,0},{144,8},{152,16},{160,24},{168,32},{176,40},{184,48},{192,... | collective-permute-start | bytes 1179656 | tf_op jit(solution)/shard_map/ppermute | solution.py:14
  14.3 54.1 %collective-permute-start.21 = (bf16[2,256,3,128]{3,1,2,0:T(8,128)(2,1)S(1)}, bf16[2,256,3,128]{3,1,2,0:T(8,128)(2,1)S(1)}, u32[]{:S(2)}, u32[]{:S(2)}) collective-permute-start(bf16[2,256,3,128]{3,1,2,0:T(8,128)(2,1)S(1)} %pad_maximum_fusion), channel_id=1, source_target_pairs={{128,0},{136,8},{144,16},{152,24},{160,32},{168,40},{176,48},{184,... | collective-permute-start | bytes 1179656 | tf_op jit(solution)/shard_map/ppermute | solution.py:14
  16.3 16.1 %all-to-all-start = ((bf16[32,24,128]{2,0,1:T(8,128)(2,1)}), bf16[32,24,128]{2,0,1:T(8,128)(2,1)S(1)}, u32[]{:S(2)}, u32[]{:S(2)}) async-start(bf16[32,24,128]{2,0,1:T(8,128)(2,1)} %copy_bitcast_fusion), calls=%async_computation | async-start | bytes 393216 | tf_op jit(solution)/shard_map/all_to_all | solution.py:42
  25.3 508.3 %all-gather.3.cloned.1.call-start = ((), (), s32[]{:S(2)}) async-start(), calls=%async_computation.1 | async-start | bytes 1769472 | tf_op jit(solution)/shard_map/all_gather | solution.py:82
  52.9 67.8 %collective-permute-start.20 = (bf16[2,256,3,128]{3,1,2,0:T(8,128)(2,1)S(1)}, bf16[2,256,3,128]{3,1,2,0:T(8,128)(2,1)S(1)}, u32[]{:S(2)}, u32[]{:S(2)}) collective-permute-start(bf16[2,256,3,128]{3,1,2,0:T(8,128)(2,1)S(1)} %pad_maximum_fusion), channel_id=1, source_target_pairs={{120,0},{128,8},{136,16},{144,24},{152,32},{160,40},{168,48},{176,... | collective-permute-start | bytes 1179656 | tf_op jit(solution)/shard_map/ppermute | solution.py:14
  61.7 61.1 %collective-permute-start.19 = (bf16[2,256,3,128]{3,1,2,0:T(8,128)(2,1)S(1)}, bf16[2,256,3,128]{3,1,2,0:T(8,128)(2,1)S(1)}, u32[]{:S(2)}, u32[]{:S(2)}) collective-permute-start(bf16[2,256,3,128]{3,1,2,0:T(8,128)(2,1)S(1)} %pad_maximum_fusion), channel_id=1, source_target_pairs={{104,0},{112,8},{120,16},{128,24},{136,32},{144,40},{152,48},{160,... | collective-permute-start | bytes 1179656 | tf_op jit(solution)/shard_map/ppermute | solution.py:14
  63.9 61.1 %collective-permute-start.18 = (bf16[2,256,3,128]{3,1,2,0:T(8,128)(2,1)S(1)}, bf16[2,256,3,128]{3,1,2,0:T(8,128)(2,1)S(1)}, u32[]{:S(2)}, u32[]{:S(2)}) collective-permute-start(bf16[2,256,3,128]{3,1,2,0:T(8,128)(2,1)S(1)} %pad_maximum_fusion), channel_id=1, source_target_pairs={{96,0},{104,8},{112,16},{120,24},{128,32},{136,40},{144,48},{152,5... | collective-permute-start | bytes 1179656 | tf_op jit(solution)/shard_map/ppermute | solution.py:14
  66.1 61.1 %collective-permute-start.17 = (bf16[2,256,3,128]{3,1,2,0:T(8,128)(2,1)S(1)}, bf16[2,256,3,128]{3,1,2,0:T(8,128)(2,1)S(1)}, u32[]{:S(2)}, u32[]{:S(2)}) collective-permute-start(bf16[2,256,3,128]{3,1,2,0:T(8,128)(2,1)S(1)} %pad_maximum_fusion), channel_id=1, source_target_pairs={{88,0},{96,8},{104,16},{112,24},{120,32},{128,40},{136,48},{144,56... | collective-permute-start | bytes 1179656 | tf_op jit(solution)/shard_map/ppermute | solution.py:14
  68.4 104.2 %collective-permute-start.16 = (bf16[2,256,3,128]{3,1,2,0:T(8,128)(2,1)S(1)}, bf16[2,256,3,128]{3,1,2,0:T(8,128)(2,1)S(1)}, u32[]{:S(2)}, u32[]{:S(2)}) collective-permute-start(bf16[2,256,3,128]{3,1,2,0:T(8,128)(2,1)S(1)} %pad_maximum_fusion), channel_id=1, source_target_pairs={{40,0},{48,8},{56,16},{64,24},{72,32},{80,40},{88,48},{96,56},{104... | collective-permute-start | bytes 1179656 | tf_op jit(solution)/shard_map/ppermute | solution.py:14
  120.7 102.5 %collective-permute-start.15 = (bf16[2,256,3,128]{3,1,2,0:T(8,128)(2,1)S(1)}, bf16[2,256,3,128]{3,1,2,0:T(8,128)(2,1)S(1)}, u32[]{:S(2)}, u32[]{:S(2)}) collective-permute-start(bf16[2,256,3,128]{3,1,2,0:T(8,128)(2,1)S(1)} %pad_maximum_fusion), channel_id=1, source_target_pairs={{32,0},{40,8},{48,16},{56,24},{64,32},{72,40},{80,48},{88,56},{96,... | collective-permute-start | bytes 1179656 | tf_op jit(solution)/shard_map/ppermute | solution.py:14
  122.8 117.0 %collective-permute-start.14 = (bf16[2,256,3,128]{3,1,2,0:T(8,128)(2,1)S(1)}, bf16[2,256,3,128]{3,1,2,0:T(8,128)(2,1)S(1)}, u32[]{:S(2)}, u32[]{:S(2)}) collective-permute-start(bf16[2,256,3,128]{3,1,2,0:T(8,128)(2,1)S(1)} %pad_maximum_fusion), channel_id=1, source_target_pairs={{24,0},{32,8},{40,16},{48,24},{56,32},{64,40},{72,48},{80,56},{88,... | collective-permute-start | bytes 1179656 | tf_op jit(solution)/shard_map/ppermute | solution.py:14
  125.0 117.1 %collective-permute-start.13 = (bf16[2,256,3,128]{3,1,2,0:T(8,128)(2,1)S(1)}, bf16[2,256,3,128]{3,1,2,0:T(8,128)(2,1)S(1)}, u32[]{:S(2)}, u32[]{:S(2)}) collective-permute-start(bf16[2,256,3,128]{3,1,2,0:T(8,128)(2,1)S(1)} %pad_maximum_fusion), channel_id=1, source_target_pairs={{8,0},{16,8},{24,16},{32,24},{40,32},{48,40},{56,48},{64,56},{72,6... | collective-permute-start | bytes 1179656 | tf_op jit(solution)/shard_map/ppermute | solution.py:14
  127.2 117.1 %collective-permute-start.12 = (bf16[2,256,3,128]{3,1,2,0:T(8,128)(2,1)S(1)}, bf16[2,256,3,128]{3,1,2,0:T(8,128)(2,1)S(1)}, u32[]{:S(2)}, u32[]{:S(2)}) collective-permute-start(bf16[2,256,3,128]{3,1,2,0:T(8,128)(2,1)S(1)} %pad_maximum_fusion), channel_id=1, source_target_pairs={{0,8},{8,16},{16,24},{24,32},{32,40},{40,48},{48,56},{56,64},{64,7... | collective-permute-start | bytes 1179656 | tf_op jit(solution)/shard_map/ppermute | solution.py:14
  172.5 87.1 %collective-permute-start.11 = (bf16[2,256,3,128]{3,1,2,0:T(8,128)(2,1)S(1)}, bf16[2,256,3,128]{3,1,2,0:T(8,128)(2,1)S(1)}, u32[]{:S(2)}, u32[]{:S(2)}) collective-permute-start(bf16[2,256,3,128]{3,1,2,0:T(8,128)(2,1)S(1)} %pad_maximum_fusion), channel_id=1, source_target_pairs={{0,24},{8,32},{16,40},{24,48},{32,56},{40,64},{48,72},{56,80},{64,... | collective-permute-start | bytes 1179656 | tf_op jit(solution)/shard_map/ppermute | solution.py:14
  223.2 56.8 %collective-permute-start.10 = (bf16[2,256,3,128]{3,1,2,0:T(8,128)(2,1)S(1)}, bf16[2,256,3,128]{3,1,2,0:T(8,128)(2,1)S(1)}, u32[]{:S(2)}, u32[]{:S(2)}) collective-permute-start(bf16[2,256,3,128]{3,1,2,0:T(8,128)(2,1)S(1)} %pad_maximum_fusion), channel_id=1, source_target_pairs={{0,32},{8,40},{16,48},{24,56},{32,64},{40,72},{48,80},{56,88},{64,... | collective-permute-start | bytes 1179656 | tf_op jit(solution)/shard_map/ppermute | solution.py:14
  239.8 58.6 %collective-permute-start.9 = (bf16[2,256,3,128]{3,1,2,0:T(8,128)(2,1)S(1)}, bf16[2,256,3,128]{3,1,2,0:T(8,128)(2,1)S(1)}, u32[]{:S(2)}, u32[]{:S(2)}) collective-permute-start(bf16[2,256,3,128]{3,1,2,0:T(8,128)(2,1)S(1)} %pad_maximum_fusion), channel_id=1, source_target_pairs={{0,40},{8,48},{16,56},{24,64},{32,72},{40,80},{48,88},{56,96},{64,... | collective-permute-start | bytes 1179656 | tf_op jit(solution)/shard_map/ppermute | solution.py:14
  242.2 87.1 %collective-permute-start.8 = (bf16[2,256,3,128]{3,1,2,0:T(8,128)(2,1)S(1)}, bf16[2,256,3,128]{3,1,2,0:T(8,128)(2,1)S(1)}, u32[]{:S(2)}, u32[]{:S(2)}) collective-permute-start(bf16[2,256,3,128]{3,1,2,0:T(8,128)(2,1)S(1)} %pad_maximum_fusion), channel_id=1, source_target_pairs={{0,88},{8,96},{16,104},{24,112},{32,120},{40,128},{48,136},{56,144... | collective-permute-start | bytes 1179656 | tf_op jit(solution)/shard_map/ppermute | solution.py:14
  244.3 104.5 %collective-permute-start.7 = (bf16[2,256,3,128]{3,1,2,0:T(8,128)(2,1)S(1)}, bf16[2,256,3,128]{3,1,2,0:T(8,128)(2,1)S(1)}, u32[]{:S(2)}, u32[]{:S(2)}) collective-permute-start(bf16[2,256,3,128]{3,1,2,0:T(8,128)(2,1)S(1)} %pad_maximum_fusion), channel_id=1, source_target_pairs={{0,96},{8,104},{16,112},{24,120},{32,128},{40,136},{48,144},{56,15... | collective-permute-start | bytes 1179656 | tf_op jit(solution)/shard_map/ppermute | solution.py:14
  259.6 94.3 %collective-permute-start.6 = (bf16[2,256,3,128]{3,1,2,0:T(8,128)(2,1)S(1)}, bf16[2,256,3,128]{3,1,2,0:T(8,128)(2,1)S(1)}, u32[]{:S(2)}, u32[]{:S(2)}) collective-permute-start(bf16[2,256,3,128]{3,1,2,0:T(8,128)(2,1)S(1)} %pad_maximum_fusion), channel_id=1, source_target_pairs={{0,104},{8,112},{16,120},{24,128},{32,136},{40,144},{48,152},{56,1... | collective-permute-start | bytes 1179656 | tf_op jit(solution)/shard_map/ppermute | solution.py:14
  279.9 85.9 %collective-permute-start.5 = (bf16[2,256,3,128]{3,1,2,0:T(8,128)(2,1)S(1)}, bf16[2,256,3,128]{3,1,2,0:T(8,128)(2,1)S(1)}, u32[]{:S(2)}, u32[]{:S(2)}) collective-permute-start(bf16[2,256,3,128]{3,1,2,0:T(8,128)(2,1)S(1)} %pad_maximum_fusion), channel_id=1, source_target_pairs={{0,120},{8,128},{16,136},{24,144},{32,152},{40,160},{48,168},{56,1... | collective-permute-start | bytes 1179656 | tf_op jit(solution)/shard_map/ppermute | solution.py:14
  298.4 78.1 %collective-permute-start.4 = (bf16[2,256,3,128]{3,1,2,0:T(8,128)(2,1)S(1)}, bf16[2,256,3,128]{3,1,2,0:T(8,128)(2,1)S(1)}, u32[]{:S(2)}, u32[]{:S(2)}) collective-permute-start(bf16[2,256,3,128]{3,1,2,0:T(8,128)(2,1)S(1)} %pad_maximum_fusion), channel_id=1, source_target_pairs={{0,128},{8,136},{16,144},{24,152},{32,160},{40,168},{48,176},{56,1... | collective-permute-start | bytes 1179656 | tf_op jit(solution)/shard_map/ppermute | solution.py:14
  329.3 48.2 %collective-permute-start.3 = (bf16[2,256,3,128]{3,1,2,0:T(8,128)(2,1)S(1)}, bf16[2,256,3,128]{3,1,2,0:T(8,128)(2,1)S(1)}, u32[]{:S(2)}, u32[]{:S(2)}) collective-permute-start(bf16[2,256,3,128]{3,1,2,0:T(8,128)(2,1)S(1)} %pad_maximum_fusion), channel_id=1, source_target_pairs={{0,136},{8,144},{16,152},{24,160},{32,168},{40,176},{48,184},{56,1... | collective-permute-start | bytes 1179656 | tf_op jit(solution)/shard_map/ppermute | solution.py:14
  348.9 29.5 %collective-permute-start.2 = (bf16[2,256,3,128]{3,1,2,0:T(8,128)(2,1)S(1)}, bf16[2,256,3,128]{3,1,2,0:T(8,128)(2,1)S(1)}, u32[]{:S(2)}, u32[]{:S(2)}) collective-permute-start(bf16[2,256,3,128]{3,1,2,0:T(8,128)(2,1)S(1)} %pad_maximum_fusion), channel_id=1, source_target_pairs={{0,152},{8,160},{16,168},{24,176},{32,184},{40,192},{48,200},{56,2... | collective-permute-start | bytes 1179656 | tf_op jit(solution)/shard_map/ppermute | solution.py:14
  354.0 26.0 %collective-permute-start.1 = (bf16[2,256,3,128]{3,1,2,0:T(8,128)(2,1)S(1)}, bf16[2,256,3,128]{3,1,2,0:T(8,128)(2,1)S(1)}, u32[]{:S(2)}, u32[]{:S(2)}) collective-permute-start(bf16[2,256,3,128]{3,1,2,0:T(8,128)(2,1)S(1)} %pad_maximum_fusion), channel_id=1, source_target_pairs={{0,160},{8,168},{16,176},{24,184},{32,192},{40,200},{48,208},{56,2... | collective-permute-start | bytes 1179656 | tf_op jit(solution)/shard_map/ppermute | solution.py:14
  365.8 36.6 %collective-permute-start = (bf16[2,256,3,128]{3,1,2,0:T(8,128)(2,1)S(1)}, bf16[2,256,3,128]{3,1,2,0:T(8,128)(2,1)S(1)}, u32[]{:S(2)}, u32[]{:S(2)}) collective-permute-start(bf16[2,256,3,128]{3,1,2,0:T(8,128)(2,1)S(1)} %pad_maximum_fusion), channel_id=1, source_target_pairs={{0,168},{8,176},{16,184},{24,192},{32,200},{40,208},{48,216},{56,2... | collective-permute-start | bytes 1179656 | tf_op jit(solution)/shard_map/ppermute | solution.py:14
  449.4 393.7 %all-gather.5.cloned.1.call-start = ((), (), s32[]{:S(2)}) async-start(), calls=%async_computation.2 | async-start | bytes 4792320 | tf_op jit(solution)/shard_map/all_gather | solution.py:85
Sparse Core Ops, SparseCore 0:
  449.5 84.0 all-gather.2
  535.6 307.3 all-gather.4
where the time goes:
time: 857 us; the launch traced here: 855 us
  waiting for transfers between devices  526 us (61%)
  starting transfers between devices  234 us (27%)
  matrix products  55.1 us (6%)
  other arithmetic  21.5 us (3%)
  between operations  14.1 us (2%)
    all_gather x1, waiting for transfers between devices, local(): lax.all_gather(out_weight, 'seq', axis=0, tiled=True)  310 us
    ppermute x26, starting transfers between devices, passed_along(): return lax.ppermute(array, axis, pairs)  225 us
    ppermute x26, waiting for transfers between devices, passed_along(): return lax.ppermute(array, axis, pairs)  127 us
    all_gather x1, waiting for transfers between devices, local(): all_heads = lax.all_gather(finished, 'head', axis=1, tiled=True)  83.4 us
    dot_general x27, matrix products, attend_block(): jnp.einsum('qhk,khd->qhd', weights.astype(jnp.bfloat16), kv_block[1], pre...  25.7 us
    dot_general x27, matrix products, attend_block(): jnp.einsum('qhd,khd->qhk', queries, kv_block[0], preferred_element_type=j...  24.4 us
    reduce_sum x14, other arithmetic, attend_block(): run_sum = run_sum * rescale + jnp.sum(weights, axis=-1)  20.6 us
  transfers between devices with their start and end apart: 29, of which 10 were waited for; matrix products, arithmetic and copies ran while one was open for 3% of the time, Pallas kernels for 0%

commit v1 on v0

--- a/solution.py
+++ b/solution.py
@@ -79,7 +79,9 @@
     run_max, run_sum, run_acc = softmax_state
     finished = (run_acc / run_sum[:, :, None]).astype(jnp.bfloat16)
     finished = finished.reshape(tile_rows, heads_dev * head_width)
-    all_heads = lax.all_gather(finished, "head", axis=1, tiled=True)
+    all_heads = jnp.concatenate(
+        lax.all_to_all(jnp.stack([finished] * lax.axis_size("head")), "head", 0, 0), axis=1
+    )
     projected = jnp.dot(
         all_heads,
         lax.all_gather(out_weight, "seq", axis=0, tiled=True),

time: 857 us -> 656 us (0.77)
  the two profiles are of different devices: /device:TPU:16 before, /device:TPU:32 now
where the time goes in v1:
time: 656 us; the launch traced here: 655 us
  waiting for transfers between devices  262 us (40%)
  starting transfers between devices  225 us (34%)
  blocking collectives  73.9 us (11%)
  matrix products  53.7 us (8%)
  other arithmetic  20.8 us (3%)
  between operations  14.1 us (2%)
    ppermute x26, starting transfers between devices, passed_along(): return lax.ppermute(array, axis, pairs)  217 us
    ppermute x26, waiting for transfers between devices, passed_along(): return lax.ppermute(array, axis, pairs)  147 us
    all_gather x1, waiting for transfers between devices, local(): lax.all_gather(out_weight, 'seq', axis=0, tiled=True)  112 us
    all_to_all x1, blocking collectives, local(): lax.all_to_all(jnp.stack([finished] * lax.axis_size('head')), 'head', 0, 0)  73.9 us
    dot_general x27, matrix products, attend_block(): jnp.einsum('qhk,khd->qhd', weights.astype(jnp.bfloat16), kv_block[1], pre...  24.9 us
    dot_general x27, matrix products, attend_block(): jnp.einsum('qhd,khd->qhk', queries, kv_block[0], preferred_element_type=j...  24.4 us
    reduce_sum x14, other arithmetic, attend_block(): run_sum = run_sum * rescale + jnp.sum(weights, axis=-1)  20.6 us
  transfers between devices with their start and end apart: 28, of which 8 were waited for; matrix products, arithmetic and copies ran while one was open for 11% of the time, Pallas kernels for 0%

profile of v1, /device:TPU:32, one launch (start us, length us, event | category | flops | bytes accessed | tf_op | source)
XLA Modules:
  0.0 654.5 jit_solution(14195702849112538360)
XLA Ops:
  6.5 1.1 copy.189
  7.8 1.1 copy.185
  9.1 1.3 collective-permute-start.25
  10.4 1.3 collective-permute-start.24
  11.7 1.3 collective-permute-start.23
  13.0 1.3 collective-permute-start.22
  14.3 1.3 collective-permute-start.21
  16.3 8.8 %all-to-all-start = ((bf16[32,24,128]{2,0,1:T(8,128)(2,1)}), bf16[32,24,128]{2,0,1:T(8,128)(2,1)S(1)}, u32[]{:S(2)}, u32[]{:S(2)}) async-start(bf16[32,24,128]{2,0,1:T(8,128)(2,1)} %copy_bitcast_fusion), calls=%async_computation | async-start | bytes 393216 | tf_op jit(solution)/shard_map/all_to_all | solution.py:42
  27.2 2.0 all-to-all-done
  29.2 1.0 fusion.329
  31.1 21.8 %collective-permute-done.25 = bf16[2,256,3,128]{3,1,2,0:T(8,128)(2,1)S(1)} collective-permute-done((bf16[2,256,3,128]{3,1,2,0:T(8,128)(2,1)S(1)}, bf16[2,256,3,128]{3,1,2,0:T(8,128)(2,1)S(1)}, u32[]{:S(2)}, u32[]{:S(2)}) %collective-permute-start.25) | collective-permute-done | bytes 393248 | tf_op jit(solution)/shard_map/ppermute | solution.py:14
  52.9 1.3 collective-permute-start.20
  54.2 1.0 fusion.303
  55.1 6.2 collective-permute-done.24
  61.3 1.3 collective-permute-start.19
  63.4 1.3 collective-permute-start.18
  64.7 1.0 fusion.305
  65.7 1.3 collective-permute-start.17
  67.9 1.3 collective-permute-start.16
  69.2 1.0 fusion.307
  70.1 59.2 %collective-permute-done.20 = bf16[2,256,3,128]{3,1,2,0:T(8,128)(2,1)S(1)} collective-permute-done((bf16[2,256,3,128]{3,1,2,0:T(8,128)(2,1)S(1)}, bf16[2,256,3,128]{3,1,2,0:T(8,128)(2,1)S(1)}, u32[]{:S(2)}, u32[]{:S(2)}) %collective-permute-start.20) | collective-permute-done | bytes 393248 | tf_op jit(solution)/shard_map/ppermute | solution.py:14
  129.3 1.3 collective-permute-start.15
  131.5 1.3 collective-permute-start.14
  133.8 1.3 collective-permute-start.13
  136.0 4.6 collective-permute-start.12
  141.5 68.9 %collective-permute-start.11 = (bf16[2,256,3,128]{3,1,2,0:T(8,128)(2,1)S(1)}, bf16[2,256,3,128]{3,1,2,0:T(8,128)(2,1)S(1)}, u32[]{:S(2)}, u32[]{:S(2)}) collective-permute-start(bf16[2,256,3,128]{3,1,2,0:T(8,128)(2,1)S(1)} %pad_maximum_fusion), channel_id=1, source_target_pairs={{0,24},{8,32},{16,40},{24,48},{32,56},{40,64},{48,72},{56,80},{64,... | collective-permute-start | bytes 1179656 | tf_op jit(solution)/shard_map/ppermute | solution.py:14
  211.2 17.1 %collective-permute-start.10 = (bf16[2,256,3,128]{3,1,2,0:T(8,128)(2,1)S(1)}, bf16[2,256,3,128]{3,1,2,0:T(8,128)(2,1)S(1)}, u32[]{:S(2)}, u32[]{:S(2)}) collective-permute-start(bf16[2,256,3,128]{3,1,2,0:T(8,128)(2,1)S(1)} %pad_maximum_fusion), channel_id=1, source_target_pairs={{0,32},{8,40},{16,48},{24,56},{32,64},{40,72},{48,80},{56,88},{64,... | collective-permute-start | bytes 1179656 | tf_op jit(solution)/shard_map/ppermute | solution.py:14
  229.2 3.8 collective-permute-start.9
  233.0 1.0 fusion.314
  234.0 1.3 collective-permute-start.8
  236.1 39.0 %collective-permute-start.7 = (bf16[2,256,3,128]{3,1,2,0:T(8,128)(2,1)S(1)}, bf16[2,256,3,128]{3,1,2,0:T(8,128)(2,1)S(1)}, u32[]{:S(2)}, u32[]{:S(2)}) collective-permute-start(bf16[2,256,3,128]{3,1,2,0:T(8,128)(2,1)S(1)} %pad_maximum_fusion), channel_id=1, source_target_pairs={{0,96},{8,104},{16,112},{24,120},{32,128},{40,136},{48,144},{56,15... | collective-permute-start | bytes 1179656 | tf_op jit(solution)/shard_map/ppermute | solution.py:14
  276.1 21.0 %collective-permute-start.6 = (bf16[2,256,3,128]{3,1,2,0:T(8,128)(2,1)S(1)}, bf16[2,256,3,128]{3,1,2,0:T(8,128)(2,1)S(1)}, u32[]{:S(2)}, u32[]{:S(2)}) collective-permute-start(bf16[2,256,3,128]{3,1,2,0:T(8,128)(2,1)S(1)} %pad_maximum_fusion), channel_id=1, source_target_pairs={{0,104},{8,112},{16,120},{24,128},{32,136},{40,144},{48,152},{56,1... | collective-permute-start | bytes 1179656 | tf_op jit(solution)/shard_map/ppermute | solution.py:14
  298.1 1.3 collective-permute-start.5
  300.3 27.2 %collective-permute-done.9 = bf16[2,256,3,128]{3,1,2,0:T(8,128)(2,1)S(1)} collective-permute-done((bf16[2,256,3,128]{3,1,2,0:T(8,128)(2,1)S(1)}, bf16[2,256,3,128]{3,1,2,0:T(8,128)(2,1)S(1)}, u32[]{:S(2)}, u32[]{:S(2)}) %collective-permute-start.9) | collective-permute-done | bytes 393248 | tf_op jit(solution)/shard_map/ppermute | solution.py:14
  327.5 1.3 collective-permute-start.4
  329.7 20.8 %collective-permute-start.3 = (bf16[2,256,3,128]{3,1,2,0:T(8,128)(2,1)S(1)}, bf16[2,256,3,128]{3,1,2,0:T(8,128)(2,1)S(1)}, u32[]{:S(2)}, u32[]{:S(2)}) collective-permute-start(bf16[2,256,3,128]{3,1,2,0:T(8,128)(2,1)S(1)} %pad_maximum_fusion), channel_id=1, source_target_pairs={{0,136},{8,144},{16,152},{24,160},{32,168},{40,176},{48,184},{56,1... | collective-permute-start | bytes 1179656 | tf_op jit(solution)/shard_map/ppermute | solution.py:14
  350.5 1.0 fusion.320
  351.5 1.3 collective-permute-start.2
  353.7 17.9 %collective-permute-start.1 = (bf16[2,256,3,128]{3,1,2,0:T(8,128)(2,1)S(1)}, bf16[2,256,3,128]{3,1,2,0:T(8,128)(2,1)S(1)}, u32[]{:S(2)}, u32[]{:S(2)}) collective-permute-start(bf16[2,256,3,128]{3,1,2,0:T(8,128)(2,1)S(1)} %pad_maximum_fusion), channel_id=1, source_target_pairs={{0,160},{8,168},{16,176},{24,184},{32,192},{40,200},{48,208},{56,2... | collective-permute-start | bytes 1179656 | tf_op jit(solution)/shard_map/ppermute | solution.py:14
  371.6 1.0 fusion.322
  372.5 23.6 %collective-permute-done.5 = bf16[2,256,3,128]{3,1,2,0:T(8,128)(2,1)S(1)} collective-permute-done((bf16[2,256,3,128]{3,1,2,0:T(8,128)(2,1)S(1)}, bf16[2,256,3,128]{3,1,2,0:T(8,128)(2,1)S(1)}, u32[]{:S(2)}, u32[]{:S(2)}) %collective-permute-start.5) | collective-permute-done | bytes 393248 | tf_op jit(solution)/shard_map/ppermute | solution.py:14
  396.2 1.5 collective-permute-start
  402.2 8.9 %collective-permute-done = bf16[2,256,3,128]{3,1,2,0:T(8,128)(2,1)S(1)} collective-permute-done((bf16[2,256,3,128]{3,1,2,0:T(8,128)(2,1)S(1)}, bf16[2,256,3,128]{3,1,2,0:T(8,128)(2,1)S(1)}, u32[]{:S(2)}, u32[]{:S(2)}) %collective-permute-start) | collective-permute-done | bytes 393248 | tf_op jit(solution)/shard_map/ppermute | solution.py:14
  412.0 1.5 fusion.159
  413.5 1.5 fusion.155
  415.0 1.6 fusion.151
  416.6 1.5 fusion.147
  418.2 1.5 fusion.143
  419.6 1.5 fusion.139
  421.1 1.4 fusion.135
  422.6 1.5 fusion.131
  424.1 1.6 fusion.127
  425.7 1.6 fusion.123
  427.3 1.5 fusion.119
  428.8 1.5 fusion.115
  430.3 1.5 fusion.111
  431.9 1.0 convolution_bitcast_fusion.1
  435.5 1.0 convolution_bitcast_fusion.5
  441.7 1.0 convolution_bitcast_fusion.12
  447.2 0.9 convolution_bitcast_fusion.18
  455.4 1.5 fusion.108
  457.0 73.9 %all_to_all.23 = bf16[8,256,384]{1,2,0:T(8,128)(2,1)S(1)} all-to-all(bf16[8,256,384]{1,2,0:T(8,128)(2,1)S(1)} %stack.7), channel_id=1, replica_groups=mesh['seq'=64,'head'=8] {'head'}, dimensions={0} | all-to-all | bytes 3145728 | tf_op jit(solution)/shard_map/all_to_all | solution.py:83
  530.9 112.3 %all-gather.2.cloned.1.call-done = bf16[3072,768]{1,0:T(8,128)(2,1)} async-done(((bf16[48,768]{1,0:T(8,128)(2,1)}), bf16[3072,768]{1,0:T(8,128)(2,1)}) %all-gather.2.cloned.1.call-update) | async-done | bytes 4718608 | tf_op jit(solution)/shard_map/all_gather | solution.py:87
  643.2 4.5 convolution_convert_fusion
  (81 shorter events, 41.5 us)
Async XLA Ops:
  6.5 9.1 %copy-start = (bf16[32,3072]{1,0:T(8,128)(2,1)S(1)}, bf16[32,3072]{1,0:T(8,128)(2,1)}, u32[]{:S(2)}) copy-start(bf16[32,3072]{1,0:T(8,128)(2,1)} %param.5) | copy-start | bytes 589828
  6.5 19.3 %copy-start.1 = (s32[1,27]{1,0:T(1,128)S(1)}, s32[1,27]{1,0:T(1,128)}, u32[]{:S(2)}) copy-start(s32[1,27]{1,0:T(1,128)} %param.8) | copy-start | bytes 328
  9.1 43.8 %collective-permute-start.25 = (bf16[2,256,3,128]{3,1,2,0:T(8,128)(2,1)S(1)}, bf16[2,256,3,128]{3,1,2,0:T(8,128)(2,1)S(1)}, u32[]{:S(2)}, u32[]{:S(2)}) collective-permute-start(bf16[2,256,3,128]{3,1,2,0:T(8,128)(2,1)S(1)} %pad_maximum_fusion), channel_id=1, source_target_pairs={{168,0},{176,8},{184,16},{192,24},{200,32},{208,40},{216,48},{224,... | collective-permute-start | bytes 1179656 | tf_op jit(solution)/shard_map/ppermute | solution.py:14
  10.4 50.9 %collective-permute-start.24 = (bf16[2,256,3,128]{3,1,2,0:T(8,128)(2,1)S(1)}, bf16[2,256,3,128]{3,1,2,0:T(8,128)(2,1)S(1)}, u32[]{:S(2)}, u32[]{:S(2)}) collective-permute-start(bf16[2,256,3,128]{3,1,2,0:T(8,128)(2,1)S(1)} %pad_maximum_fusion), channel_id=1, source_target_pairs={{160,0},{168,8},{176,16},{184,24},{192,32},{200,40},{208,48},{216,... | collective-permute-start | bytes 1179656 | tf_op jit(solution)/shard_map/ppermute | solution.py:14
  11.7 51.8 %collective-permute-start.23 = (bf16[2,256,3,128]{3,1,2,0:T(8,128)(2,1)S(1)}, bf16[2,256,3,128]{3,1,2,0:T(8,128)(2,1)S(1)}, u32[]{:S(2)}, u32[]{:S(2)}) collective-permute-start(bf16[2,256,3,128]{3,1,2,0:T(8,128)(2,1)S(1)} %pad_maximum_fusion), channel_id=1, source_target_pairs={{152,0},{160,8},{168,16},{176,24},{184,32},{192,40},{200,48},{208,... | collective-permute-start | bytes 1179656 | tf_op jit(solution)/shard_map/ppermute | solution.py:14
  13.0 52.7 %collective-permute-start.22 = (bf16[2,256,3,128]{3,1,2,0:T(8,128)(2,1)S(1)}, bf16[2,256,3,128]{3,1,2,0:T(8,128)(2,1)S(1)}, u32[]{:S(2)}, u32[]{:S(2)}) collective-permute-start(bf16[2,256,3,128]{3,1,2,0:T(8,128)(2,1)S(1)} %pad_maximum_fusion), channel_id=1, source_target_pairs={{136,0},{144,8},{152,16},{160,24},{168,32},{176,40},{184,48},{192,... | collective-permute-start | bytes 1179656 | tf_op jit(solution)/shard_map/ppermute | solution.py:14
  14.3 53.6 %collective-permute-start.21 = (bf16[2,256,3,128]{3,1,2,0:T(8,128)(2,1)S(1)}, bf16[2,256,3,128]{3,1,2,0:T(8,128)(2,1)S(1)}, u32[]{:S(2)}, u32[]{:S(2)}) collective-permute-start(bf16[2,256,3,128]{3,1,2,0:T(8,128)(2,1)S(1)} %pad_maximum_fusion), channel_id=1, source_target_pairs={{128,0},{136,8},{144,16},{152,24},{160,32},{168,40},{176,48},{184,... | collective-permute-start | bytes 1179656 | tf_op jit(solution)/shard_map/ppermute | solution.py:14
  16.3 12.9 %all-to-all-start = ((bf16[32,24,128]{2,0,1:T(8,128)(2,1)}), bf16[32,24,128]{2,0,1:T(8,128)(2,1)S(1)}, u32[]{:S(2)}, u32[]{:S(2)}) async-start(bf16[32,24,128]{2,0,1:T(8,128)(2,1)} %copy_bitcast_fusion), calls=%async_computation | async-start | bytes 393216 | tf_op jit(solution)/shard_map/all_to_all | solution.py:42
  25.1 618.1 %all-gather.2.cloned.1.call-start = ((), (), s32[]{:S(2)}) async-start(), calls=%async_computation.2 | async-start | bytes 4792320 | tf_op jit(solution)/shard_map/all_gather | solution.py:87
  52.9 76.5 %collective-permute-start.20 = (bf16[2,256,3,128]{3,1,2,0:T(8,128)(2,1)S(1)}, bf16[2,256,3,128]{3,1,2,0:T(8,128)(2,1)S(1)}, u32[]{:S(2)}, u32[]{:S(2)}) collective-permute-start(bf16[2,256,3,128]{3,1,2,0:T(8,128)(2,1)S(1)} %pad_maximum_fusion), channel_id=1, source_target_pairs={{120,0},{128,8},{136,16},{144,24},{152,32},{160,40},{168,48},{176,... | collective-permute-start | bytes 1179656 | tf_op jit(solution)/shard_map/ppermute | solution.py:14
  61.3 70.2 %collective-permute-start.19 = (bf16[2,256,3,128]{3,1,2,0:T(8,128)(2,1)S(1)}, bf16[2,256,3,128]{3,1,2,0:T(8,128)(2,1)S(1)}, u32[]{:S(2)}, u32[]{:S(2)}) collective-permute-start(bf16[2,256,3,128]{3,1,2,0:T(8,128)(2,1)S(1)} %pad_maximum_fusion), channel_id=1, source_target_pairs={{104,0},{112,8},{120,16},{128,24},{136,32},{144,40},{152,48},{160,... | collective-permute-start | bytes 1179656 | tf_op jit(solution)/shard_map/ppermute | solution.py:14
  63.4 70.3 %collective-permute-start.18 = (bf16[2,256,3,128]{3,1,2,0:T(8,128)(2,1)S(1)}, bf16[2,256,3,128]{3,1,2,0:T(8,128)(2,1)S(1)}, u32[]{:S(2)}, u32[]{:S(2)}) collective-permute-start(bf16[2,256,3,128]{3,1,2,0:T(8,128)(2,1)S(1)} %pad_maximum_fusion), channel_id=1, source_target_pairs={{96,0},{104,8},{112,16},{120,24},{128,32},{136,40},{144,48},{152,5... | collective-permute-start | bytes 1179656 | tf_op jit(solution)/shard_map/ppermute | solution.py:14
  65.7 70.3 %collective-permute-start.17 = (bf16[2,256,3,128]{3,1,2,0:T(8,128)(2,1)S(1)}, bf16[2,256,3,128]{3,1,2,0:T(8,128)(2,1)S(1)}, u32[]{:S(2)}, u32[]{:S(2)}) collective-permute-start(bf16[2,256,3,128]{3,1,2,0:T(8,128)(2,1)S(1)} %pad_maximum_fusion), channel_id=1, source_target_pairs={{88,0},{96,8},{104,16},{112,24},{120,32},{128,40},{136,48},{144,56... | collective-permute-start | bytes 1179656 | tf_op jit(solution)/shard_map/ppermute | solution.py:14
  67.9 73.6 %collective-permute-start.16 = (bf16[2,256,3,128]{3,1,2,0:T(8,128)(2,1)S(1)}, bf16[2,256,3,128]{3,1,2,0:T(8,128)(2,1)S(1)}, u32[]{:S(2)}, u32[]{:S(2)}) collective-permute-start(bf16[2,256,3,128]{3,1,2,0:T(8,128)(2,1)S(1)} %pad_maximum_fusion), channel_id=1, source_target_pairs={{40,0},{48,8},{56,16},{64,24},{72,32},{80,40},{88,48},{96,56},{104... | collective-permute-start | bytes 1179656 | tf_op jit(solution)/shard_map/ppermute | solution.py:14
  129.3 81.9 %collective-permute-start.15 = (bf16[2,256,3,128]{3,1,2,0:T(8,128)(2,1)S(1)}, bf16[2,256,3,128]{3,1,2,0:T(8,128)(2,1)S(1)}, u32[]{:S(2)}, u32[]{:S(2)}) collective-permute-start(bf16[2,256,3,128]{3,1,2,0:T(8,128)(2,1)S(1)} %pad_maximum_fusion), channel_id=1, source_target_pairs={{32,0},{40,8},{48,16},{56,24},{64,32},{72,40},{80,48},{88,56},{96,... | collective-permute-start | bytes 1179656 | tf_op jit(solution)/shard_map/ppermute | solution.py:14
  131.5 97.6 %collective-permute-start.14 = (bf16[2,256,3,128]{3,1,2,0:T(8,128)(2,1)S(1)}, bf16[2,256,3,128]{3,1,2,0:T(8,128)(2,1)S(1)}, u32[]{:S(2)}, u32[]{:S(2)}) collective-permute-start(bf16[2,256,3,128]{3,1,2,0:T(8,128)(2,1)S(1)} %pad_maximum_fusion), channel_id=1, source_target_pairs={{24,0},{32,8},{40,16},{48,24},{56,32},{64,40},{72,48},{80,56},{88,... | collective-permute-start | bytes 1179656 | tf_op jit(solution)/shard_map/ppermute | solution.py:14
  133.8 100.2 %collective-permute-start.13 = (bf16[2,256,3,128]{3,1,2,0:T(8,128)(2,1)S(1)}, bf16[2,256,3,128]{3,1,2,0:T(8,128)(2,1)S(1)}, u32[]{:S(2)}, u32[]{:S(2)}) collective-permute-start(bf16[2,256,3,128]{3,1,2,0:T(8,128)(2,1)S(1)} %pad_maximum_fusion), channel_id=1, source_target_pairs={{8,0},{16,8},{24,16},{32,24},{40,32},{48,40},{56,48},{64,56},{72,6... | collective-permute-start | bytes 1179656 | tf_op jit(solution)/shard_map/ppermute | solution.py:14
  136.0 100.2 %collective-permute-start.12 = (bf16[2,256,3,128]{3,1,2,0:T(8,128)(2,1)S(1)}, bf16[2,256,3,128]{3,1,2,0:T(8,128)(2,1)S(1)}, u32[]{:S(2)}, u32[]{:S(2)}) collective-permute-start(bf16[2,256,3,128]{3,1,2,0:T(8,128)(2,1)S(1)} %pad_maximum_fusion), channel_id=1, source_target_pairs={{0,8},{8,16},{16,24},{24,32},{32,40},{40,48},{48,56},{56,64},{64,7... | collective-permute-start | bytes 1179656 | tf_op jit(solution)/shard_map/ppermute | solution.py:14
  141.5 134.6 %collective-permute-start.11 = (bf16[2,256,3,128]{3,1,2,0:T(8,128)(2,1)S(1)}, bf16[2,256,3,128]{3,1,2,0:T(8,128)(2,1)S(1)}, u32[]{:S(2)}, u32[]{:S(2)}) collective-permute-start(bf16[2,256,3,128]{3,1,2,0:T(8,128)(2,1)S(1)} %pad_maximum_fusion), channel_id=1, source_target_pairs={{0,24},{8,32},{16,40},{24,48},{32,56},{40,64},{48,72},{56,80},{64,... | collective-permute-start | bytes 1179656 | tf_op jit(solution)/shard_map/ppermute | solution.py:14
  211.2 86.9 %collective-permute-start.10 = (bf16[2,256,3,128]{3,1,2,0:T(8,128)(2,1)S(1)}, bf16[2,256,3,128]{3,1,2,0:T(8,128)(2,1)S(1)}, u32[]{:S(2)}, u32[]{:S(2)}) collective-permute-start(bf16[2,256,3,128]{3,1,2,0:T(8,128)(2,1)S(1)} %pad_maximum_fusion), channel_id=1, source_target_pairs={{0,32},{8,40},{16,48},{24,56},{32,64},{40,72},{48,80},{56,88},{64,... | collective-permute-start | bytes 1179656 | tf_op jit(solution)/shard_map/ppermute | solution.py:14
  229.2 98.3 %collective-permute-start.9 = (bf16[2,256,3,128]{3,1,2,0:T(8,128)(2,1)S(1)}, bf16[2,256,3,128]{3,1,2,0:T(8,128)(2,1)S(1)}, u32[]{:S(2)}, u32[]{:S(2)}) collective-permute-start(bf16[2,256,3,128]{3,1,2,0:T(8,128)(2,1)S(1)} %pad_maximum_fusion), channel_id=1, source_target_pairs={{0,40},{8,48},{16,56},{24,64},{32,72},{40,80},{48,88},{56,96},{64,... | collective-permute-start | bytes 1179656 | tf_op jit(solution)/shard_map/ppermute | solution.py:14
  234.0 95.7 %collective-permute-start.8 = (bf16[2,256,3,128]{3,1,2,0:T(8,128)(2,1)S(1)}, bf16[2,256,3,128]{3,1,2,0:T(8,128)(2,1)S(1)}, u32[]{:S(2)}, u32[]{:S(2)}) collective-permute-start(bf16[2,256,3,128]{3,1,2,0:T(8,128)(2,1)S(1)} %pad_maximum_fusion), channel_id=1, source_target_pairs={{0,88},{8,96},{16,104},{24,112},{32,120},{40,128},{48,136},{56,144... | collective-permute-start | bytes 1179656 | tf_op jit(solution)/shard_map/ppermute | solution.py:14
  236.1 115.3 %collective-permute-start.7 = (bf16[2,256,3,128]{3,1,2,0:T(8,128)(2,1)S(1)}, bf16[2,256,3,128]{3,1,2,0:T(8,128)(2,1)S(1)}, u32[]{:S(2)}, u32[]{:S(2)}) collective-permute-start(bf16[2,256,3,128]{3,1,2,0:T(8,128)(2,1)S(1)} %pad_maximum_fusion), channel_id=1, source_target_pairs={{0,96},{8,104},{16,112},{24,120},{32,128},{40,136},{48,144},{56,15... | collective-permute-start | bytes 1179656 | tf_op jit(solution)/shard_map/ppermute | solution.py:14
  276.1 77.6 %collective-permute-start.6 = (bf16[2,256,3,128]{3,1,2,0:T(8,128)(2,1)S(1)}, bf16[2,256,3,128]{3,1,2,0:T(8,128)(2,1)S(1)}, u32[]{:S(2)}, u32[]{:S(2)}) collective-permute-start(bf16[2,256,3,128]{3,1,2,0:T(8,128)(2,1)S(1)} %pad_maximum_fusion), channel_id=1, source_target_pairs={{0,104},{8,112},{16,120},{24,128},{32,136},{40,144},{48,152},{56,1... | collective-permute-start | bytes 1179656 | tf_op jit(solution)/shard_map/ppermute | solution.py:14
  298.1 98.1 %collective-permute-start.5 = (bf16[2,256,3,128]{3,1,2,0:T(8,128)(2,1)S(1)}, bf16[2,256,3,128]{3,1,2,0:T(8,128)(2,1)S(1)}, u32[]{:S(2)}, u32[]{:S(2)}) collective-permute-start(bf16[2,256,3,128]{3,1,2,0:T(8,128)(2,1)S(1)} %pad_maximum_fusion), channel_id=1, source_target_pairs={{0,120},{8,128},{16,136},{24,144},{32,152},{40,160},{48,168},{56,1... | collective-permute-start | bytes 1179656 | tf_op jit(solution)/shard_map/ppermute | solution.py:14
  327.5 71.0 %collective-permute-start.4 = (bf16[2,256,3,128]{3,1,2,0:T(8,128)(2,1)S(1)}, bf16[2,256,3,128]{3,1,2,0:T(8,128)(2,1)S(1)}, u32[]{:S(2)}, u32[]{:S(2)}) collective-permute-start(bf16[2,256,3,128]{3,1,2,0:T(8,128)(2,1)S(1)} %pad_maximum_fusion), channel_id=1, source_target_pairs={{0,128},{8,136},{16,144},{24,152},{32,160},{40,168},{48,176},{56,1... | collective-permute-start | bytes 1179656 | tf_op jit(solution)/shard_map/ppermute | solution.py:14
  329.7 69.7 %collective-permute-start.3 = (bf16[2,256,3,128]{3,1,2,0:T(8,128)(2,1)S(1)}, bf16[2,256,3,128]{3,1,2,0:T(8,128)(2,1)S(1)}, u32[]{:S(2)}, u32[]{:S(2)}) collective-permute-start(bf16[2,256,3,128]{3,1,2,0:T(8,128)(2,1)S(1)} %pad_maximum_fusion), channel_id=1, source_target_pairs={{0,136},{8,144},{16,152},{24,160},{32,168},{40,176},{48,184},{56,1... | collective-permute-start | bytes 1179656 | tf_op jit(solution)/shard_map/ppermute | solution.py:14
  351.5 48.9 %collective-permute-start.2 = (bf16[2,256,3,128]{3,1,2,0:T(8,128)(2,1)S(1)}, bf16[2,256,3,128]{3,1,2,0:T(8,128)(2,1)S(1)}, u32[]{:S(2)}, u32[]{:S(2)}) collective-permute-start(bf16[2,256,3,128]{3,1,2,0:T(8,128)(2,1)S(1)} %pad_maximum_fusion), channel_id=1, source_target_pairs={{0,152},{8,160},{16,168},{24,176},{32,184},{40,192},{48,200},{56,2... | collective-permute-start | bytes 1179656 | tf_op jit(solution)/shard_map/ppermute | solution.py:14
  353.7 47.5 %collective-permute-start.1 = (bf16[2,256,3,128]{3,1,2,0:T(8,128)(2,1)S(1)}, bf16[2,256,3,128]{3,1,2,0:T(8,128)(2,1)S(1)}, u32[]{:S(2)}, u32[]{:S(2)}) collective-permute-start(bf16[2,256,3,128]{3,1,2,0:T(8,128)(2,1)S(1)} %pad_maximum_fusion), channel_id=1, source_target_pairs={{0,160},{8,168},{16,176},{24,184},{32,192},{40,200},{48,208},{56,2... | collective-permute-start | bytes 1179656 | tf_op jit(solution)/shard_map/ppermute | solution.py:14
  396.2 15.0 %collective-permute-start = (bf16[2,256,3,128]{3,1,2,0:T(8,128)(2,1)S(1)}, bf16[2,256,3,128]{3,1,2,0:T(8,128)(2,1)S(1)}, u32[]{:S(2)}, u32[]{:S(2)}) collective-permute-start(bf16[2,256,3,128]{3,1,2,0:T(8,128)(2,1)S(1)} %pad_maximum_fusion), channel_id=1, source_target_pairs={{0,168},{8,176},{16,184},{24,192},{32,200},{40,208},{48,216},{56,2... | collective-permute-start | bytes 1179656 | tf_op jit(solution)/shard_map/ppermute | solution.py:14
Sparse Core Ops, SparseCore 0:
  28.0 615.1 all-gather.1
